TPU v7x, 32 devices: a whole 2x2x4 slice. The times are simulated.
32 devices in a mesh: tm: 4 (over y, x), space: 2 (over core), ens: 4 (over z).
Axes of the slice: x: 2, y: 2, z: 4, core: 2. Of those that a mesh axis runs over, the one named last changes fastest.
Arguments:
- initial_state: float32 [4, 4, 32, 512], P('ens', None, 'space'), may hold values from -6 to 6
- forcing: float32 [2, 32, 512], P(None, 'space'), may hold values from -6 to 6
- w_down: bfloat16 [128, 16], replicated, may hold values from -1.5 to 1.5
- depth_kernel: float32 [2, 128, 9], replicated, may hold values from -2 to 2
- w_point: bfloat16 [2, 128, 128], replicated, may hold values from -0.5 to 0.5
- w_up: bfloat16 [16, 128], replicated, may hold values from -0.25 to 0.25
Outputs:
- slice_ends: float32 [4, 4, 4, 32, 512], P('ens', 'tm', None, 'space')
- ensemble_mean: float32 [4, 4, 32, 512], P('tm', None, 'space')
All inputs are finite; a program needn't handle non-finite values.
Results may differ from a plain program's by a relative error of at most 0.0084.
Values may be sent and summed in bfloat16 or wider, within the bound.
A program may use at most 64 MiB of HBM per device.

v0:
```python
import jax
import jax.numpy as jnp
from jax import lax
from jax.experimental import pallas as pl
from jax.experimental.pallas import tpu as pltpu
from jax.sharding import PartitionSpec as P

TIME_STEP = 0.05
VISCOSITY = 0.5
DIFFUSIVITY = 0.3
FINE = 4
MESH = pl.DeviceIdType.MESH
F32 = jnp.float32
BF16 = jnp.bfloat16


def swap_order(p):
    return p + lax.div(p, 2) * (1 - 2 * lax.rem(p, 2))


def iota(shape, dim):
    return lax.broadcasted_iota(jnp.int32, shape, dim)


def split3(x):
    hi = x.astype(BF16)
    rest = x - hi.astype(F32)
    mid = rest.astype(BF16)
    low = (rest - mid.astype(F32)).astype(BF16)
    return jnp.concatenate([hi, mid, low], axis=0)


def exact_move(x, pick):
    rows = x.shape[0]
    y = jnp.dot(split3(x), pick, preferred_element_type=F32)
    return y[:rows] + y[rows : 2 * rows] + y[2 * rows :]


def fine_sweep(state, force):
    cur = state
    rows = cur.shape[1]
    fields = cur.shape[0] // 2
    for _ in range(FINE):
        north = pltpu.roll(cur, 1, 1)
        south = pltpu.roll(cur, rows - 1, 1)
        down = (south - north) * 0.5
        vert = south + north - 4.0 * cur
        out = [None] * (2 * fields)
        for b in (0, 1):
            across, lap = [], []
            for f in range(fields):
                ev, od = cur[2 * f], cur[2 * f + 1]
                cols = ev.shape[1]
                if b == 0:
                    east, west = od, pltpu.roll(od, 1, 1)
                else:
                    east, west = pltpu.roll(ev, cols - 1, 1), ev
                across.append((east - west) * 0.5)
                lap.append(vert[2 * f + b] + east + west)
            u, v = cur[b], cur[2 + b]

            def carried(f):
                return u * across[f] + v * down[2 * f + b]

            rates = [
                VISCOSITY * lap[0] - carried(0) - across[2] + force[b],
                VISCOSITY * lap[1] - carried(1) - down[4 + b] + force[2 + b],
                VISCOSITY * lap[2] - (across[0] + down[2 + b]),
                DIFFUSIVITY * lap[3] - carried(3),
            ]
            for f in range(fields):
                out[2 * f + b] = cur[2 * f + b] + TIME_STEP * rates[f]
        cur = jnp.stack(out)
    return cur


def gelu(x):
    return 0.5 * x * (1.0 + jnp.tanh(0.7978845608028654 * (x + 0.044715 * x * x * x)))


def kernel(tm, spaces, u_ref, f_ref, wd_ref, kt_ref, wp_ref, wu_ref, ends_ref,
           wdb, wub, wcs, snd0, nrt0, sth0, snd, nrt, sth, send_sem, recv_sem):
    t = lax.axis_index("tm")
    s = lax.axis_index("space")
    fields, half, columns = u_ref.shape
    cols = columns // 2
    block = half // tm
    ch = wd_ref.shape[0]
    layers = wp_ref.shape[0]
    groups = 2 * fields
    padded = 4 * block
    pos = swap_order(t)
    ring = s * tm + pos
    total = tm * spaces
    neighbours = []
    for step in (total - 1, 1):
        g = lax.rem(ring + step, total)
        neighbours.append({"tm": swap_order(lax.rem(g, tm)), "space": lax.div(g, tm)})
    to_north, to_south = neighbours

    def exchange(stage, src, from_north, from_south):
        copies = [
            pltpu.make_async_remote_copy(src, from_south, send_sem.at[stage, 0], recv_sem.at[stage, 0],
                                         device_id=to_north, device_id_type=MESH),
            pltpu.make_async_remote_copy(src, from_north, send_sem.at[stage, 1], recv_sem.at[stage, 1],
                                         device_id=to_south, device_id_type=MESH),
        ]
        for c in copies:
            c.start()
        return copies

    def own_rows(ref):
        picked = ref[:, 0:block, :]
        for k in range(1, tm):
            picked = jnp.where(pos == k, ref[:, k * block : (k + 1) * block, :], picked)
        return picked

    r_i, c_i = iota((columns, columns), 0), iota((columns, columns), 1)
    odd = jnp.where(c_i >= cols, 1, 0)
    to_parity = jnp.where(r_i == 2 * (c_i - odd * cols) + odd, 1.0, 0.0).astype(BF16)
    both = jnp.concatenate([own_rows(u_ref), own_rows(f_ref)], axis=0)
    count = fields + f_ref.shape[0]
    moved = exact_move(both.reshape(count * block, columns), to_parity).reshape(count, block, columns)
    for f in range(count):
        for b in (0, 1):
            snd0[2 * f + b] = moved[f, :, b * cols : (b + 1) * cols]
    copies = exchange(0, snd0, nrt0, sth0)

    rows_in = 3 * block // 2
    wide = groups * padded
    for r in range(rows_in):
        q, k = iota((2 * groups, wide), 0), iota((2 * groups, wide), 1)
        fq, aq, bq = q // 4, (q // 2) % 2, q % 2
        gk, rk = k // padded, k % padded
        sel = jnp.where((gk == 2 * fq + bq) & (rk == 2 * r + aq), 1.0, 0.0).astype(BF16)
        wdb[r * ch : (r + 1) * ch] = jnp.dot(wd_ref[...], sel, preferred_element_type=F32).astype(BF16)
    small = groups * block
    for r in range(block // 2):
        q, k = iota((small, 2 * groups), 1), iota((small, 2 * groups), 0)
        fq, aq, bq = q // 4, (q // 2) % 2, q % 2
        gk, rk = k // block, k % block
        sel = jnp.where((gk == 2 * fq + bq) & (rk == 2 * r + aq), 1.0, 0.0).astype(BF16)
        wub[:, r * ch : (r + 1) * ch] = jnp.dot(sel, wu_ref[...], preferred_element_type=F32).astype(BF16)
    for l in range(layers):
        w = wp_ref[l].astype(F32)
        for a in range(3):
            for b in range(3):
                tap = kt_ref[l, 3 * a + b : 3 * a + b + 1, :]
                wcs[l, b * ch : (b + 1) * ch, a * ch : (a + 1) * ch] = (w * tap).astype(BF16)

    def coarse(own, state):
        x = state.astype(BF16).reshape(wide, cols)
        hidden = jnp.dot(wdb[...], x, preferred_element_type=F32).astype(BF16)
        for l in range(layers):
            n_out = hidden.shape[0] // ch - 2
            new = []
            for r in range(n_out):
                y = jnp.dot(wcs[l], hidden[r * ch : (r + 3) * ch], preferred_element_type=F32)
                lifted = y[ch : 2 * ch] + pltpu.roll(y[:ch], 1, 1) + pltpu.roll(y[2 * ch :], cols - 1, 1)
                old = hidden[(r + 1) * ch : (r + 2) * ch].astype(F32)
                new.append((old + gelu(lifted)).astype(BF16))
            hidden = jnp.concatenate(new, axis=0)
        delta = jnp.dot(wub[...], hidden, preferred_element_type=F32)
        return own + delta.reshape(groups, block, cols)

    def fine(state):
        return fine_sweep(state, force)[:, block : 2 * block]

    def pad(north, own, south):
        return jnp.concatenate([north, own, south, jnp.zeros_like(own)], axis=1)

    r_j, c_j = iota((columns, columns), 0), iota((columns, columns), 1)
    odd_j = jnp.where(r_j >= cols, 1, 0)
    from_parity = jnp.where(c_j == 2 * (r_j - odd_j * cols) + odd_j, 1.0, 0.0).astype(BF16)

    def finish(n, end):
        pieces = [jnp.concatenate([end[2 * f], end[2 * f + 1]], axis=1) for f in range(fields)]
        flat = jnp.concatenate(pieces, axis=0)
        ends_ref[n] = exact_move(flat, from_parity).reshape(fields, block, columns)

    def next_stage(stage, starts):
        for i, start in enumerate(starts):
            snd[stage - 1, i] = start
        k = len(starts)
        return exchange(stage, snd.at[stage - 1, 0:k], nrt.at[stage - 1, 0:k], sth.at[stage - 1, 0:k])

    def arrived(stage, moving, starts):
        for c in moving:
            c.wait()
        return [pad(nrt[stage - 1, i], start, sth[stage - 1, i]) for i, start in enumerate(starts)]

    for c in copies:
        c.wait()
    everything = pad(nrt0[...], snd0[...], sth0[...])
    force = everything[groups:]
    start0 = snd0[0:groups]
    state0 = everything[:groups]

    g0 = coarse(start0, state0)
    v1 = g0 + (fine(state0) - g0)
    u1 = g0
    moving = next_stage(1, [u1, v1])
    finish(0, v1)
    u1p, v1p = arrived(1, moving, [u1, v1])

    u2 = coarse(u1, u1p)
    gv1 = coarse(v1, v1p)
    v2 = gv1 + (fine(u1p) - u2)
    w2 = gv1 + (fine(v1p) - gv1)
    moving = next_stage(2, [u2, v2, w2])
    finish(1, w2)
    u2p, v2p, w2p = arrived(2, moving, [u2, v2, w2])

    gu2 = coarse(u2, u2p)
    gv2 = coarse(v2, v2p)
    gw2 = coarse(w2, w2p)
    v3 = gv2 + (fine(u2p) - gu2)
    w3 = gw2 + (fine(v2p) - gv2)
    moving = next_stage(3, [v3, w3])
    finish(2, w3)
    v3p, w3p = arrived(3, moving, [v3, w3])

    gv3 = coarse(v3, v3p)
    gw3 = coarse(w3, w3p)
    finish(3, gw3 + (fine(v3p) - gv3))


def local(initial_state, forcing, w_down, depth_kernel, w_point, w_up):
    tm, spaces = lax.axis_size("tm"), lax.axis_size("space")
    _, fields, half, columns = initial_state.shape
    block = half // tm
    cols, groups = columns // 2, 2 * fields
    layers, ch, _ = depth_kernel.shape
    assert block == FINE == 2 * layers and tm == 4
    taps = jnp.swapaxes(depth_kernel, 1, 2)
    count = groups + 2 * forcing.shape[0]
    vmem = pl.BlockSpec(memory_space=pltpu.VMEM)
    ends = pl.pallas_call(
        lambda *refs: kernel(tm, spaces, *refs),
        name="parareal",
        out_shape=jax.ShapeDtypeStruct((tm, fields, block, columns), F32),
        in_specs=[vmem] * 6,
        out_specs=vmem,
        scratch_shapes=[
            pltpu.VMEM((3 * block // 2 * ch, groups * 4 * block), BF16),
            pltpu.VMEM((groups * block, block // 2 * ch), BF16),
            pltpu.VMEM((layers, 3 * ch, 3 * ch), BF16),
            pltpu.VMEM((count, block, cols), F32),
            pltpu.VMEM((count, block, cols), F32),
            pltpu.VMEM((count, block, cols), F32),
            pltpu.VMEM((3, 3, groups, block, cols), F32),
            pltpu.VMEM((3, 3, groups, block, cols), F32),
            pltpu.VMEM((3, 3, groups, block, cols), F32),
            pltpu.SemaphoreType.DMA((4, 2)),
            pltpu.SemaphoreType.DMA((4, 2)),
        ],
        compiler_params=pltpu.CompilerParams(has_side_effects=True, vmem_limit_bytes=32 << 20),
    )(initial_state[0], forcing, w_down, taps, w_point, w_up)
    gathered = lax.all_to_all(ends, "tm", 0, 0)
    order = jnp.stack([gathered[p] for p in (0, 1, 3, 2)], axis=1)
    ending = order.reshape(fields, half, columns)
    mean = lax.psum(ending, "ens") / lax.axis_size("ens")
    return ending[None, None], mean[None]


def solution(mesh):
    in_specs = (P("ens", None, "space", None), P(None, "space", None), P(), P(), P(), P())
    out_specs = (P("ens", "tm", None, "space", None), P("tm", None, "space", None))
    return jax.shard_map(local, mesh=mesh, in_specs=in_specs, out_specs=out_specs, check_vma=False)
```

profile of v0, /device:TPU:6, one launch (start us, length us, event | category | flops | bytes accessed | tf_op | source)
XLA Modules:
  0.0 99.3 jit_solution(13508427333216385541)
XLA Ops:
  7.2 0.0 copy-start.1
  7.2 0.7 copy.17
  7.9 0.8 copy.11.refs_2_
  8.7 0.0 copy-done.1
  8.7 0.0 copy-start
  8.7 0.9 copy-done
  9.6 0.0 copy-start.2
  9.6 0.8 copy-done.2
  10.5 0.0 copy-start.3
  10.5 0.7 copy-done.3
  11.2 32.8 %parareal.1 = f32[4,4,4,512]{3,2,1,0:T(4,128)S(1)} custom-call(f32[4,16,512]{2,1,0:T(8,128)S(1)} %bitcast.16, f32[2,16,512]{2,1,0:T(8,128)S(1)} %copy-done.1, bf16[128,16]{1,0:T(8,128)(2,1)S(1)} %copy.11.refs_2_, f32[2,9,128]{2,1,0:T(8,128)S(1)} %bitcast.17, bf16[2,128,128]{2,1,0:T(8,128)(2,1)S(1)} %copy-done.2, bf16[16,128]{1,0:T(8,128)(2,1)S(1)} %copy-done.3), custom_call_target="tpu_custom_call" | custom-call | tf_op jit(solution)/shard_map/parareal/pallas_call | solution.py:238
  43.9 6.8 %all_to_all.5 = f32[4,4,4,512]{3,2,1,0:T(4,128)S(1)} all-to-all(f32[4,4,4,512]{3,2,1,0:T(4,128)S(1)} %parareal.1), channel_id=1, replica_groups=mesh['tm'=4,'space'=2,'ens'=4] {'tm'}, dimensions={0} | all-to-all | bytes 262144 | tf_op jit(solution)/shard_map/all_to_all | solution.py:259
  50.8 0.1 copy.12
  50.8 0.0 copy-start.4
  50.9 0.7 copy.14
  51.6 0.0 copy-done.4
  51.6 0.0 all-reduce.2.cloned.1.call-start
  51.6 0.7 all-reduce.2.cloned.1.call-update
  52.3 38.6 %all-reduce.2.cloned.1.call-done = f32[4,16,512]{2,0,1:T(4,128)} async-done(((f32[4,16,512]{2,0,1:T(4,128)}), f32[4,16,512]{2,0,1:T(4,128)}) %all-reduce.2.cloned.1.call-update) | async-done | bytes 131088 | tf_op jit(solution)/shard_map/psum | solution.py:262
  90.9 0.9 multiply_bitcast_fusion
  91.8 0.7 copy.15
  (2 shorter events, 0.0 us)
Async XLA Ops:
  7.2 1.5 %copy-start.1 = (f32[2,16,512]{2,1,0:T(8,128)S(1)}, f32[2,16,512]{2,1,0:T(8,128)}, u32[]{:S(2)}) copy-start(f32[2,16,512]{2,1,0:T(8,128)} %refs_1_.1) | copy-start | bytes 196612
  8.7 0.9 copy-start
  9.6 0.8 copy-start.2
  10.5 0.7 copy-start.3
  50.8 0.7 copy-start.4
  51.6 39.3 %all-reduce.2.cloned.1.call-start = ((), (), s32[]{:S(2)}) async-start(), calls=%async_computation.1 | async-start | bytes 262144 | tf_op jit(solution)/shard_map/psum | solution.py:262
Sparse Core Ops, SparseCore 0:
  55.3 35.5 all-reduce.1
where the time goes:
time: 101 us; the launch traced here: 99.3 us
  waiting for transfers between devices  39.3 us (39%)
  Pallas kernels  32.8 us (32%)
  between operations  14.1 us (14%)
  blocking collectives  6.79 us (7%)
  local copies, waits for them, and re-layouts  5.44 us (5%)
    psum x1, waiting for transfers between devices, local(): mean = lax.psum(ending, 'ens') / lax.axis_size('ens')  38.6 us
    pallas_call x1, Pallas kernels, local(): pl.pallas_call(lambda *refs: kernel(tm, spaces, *refs), name='parareal',...  32.8 us
    all_to_all x1, blocking collectives, local(): gathered = lax.all_to_all(ends, 'tm', 0, 0)  6.79 us
    unnamed x14, local copies, waits for them, and re-layouts  5.38 us
  transfers between devices with their start and end apart: 1, of which 1 were waited for; matrix products, arithmetic and copies ran while one was open for 0% of the time, Pallas kernels for 0%

commit v1 on v0

--- a/solution.py
+++ b/solution.py
@@ -15,6 +15,8 @@
 
 
 def swap_order(p):
+    if isinstance(p, int):
+        return p + (p // 2) * (1 - 2 * (p % 2))
     return p + lax.div(p, 2) * (1 - 2 * lax.rem(p, 2))
 
 
@@ -78,8 +80,19 @@
     return 0.5 * x * (1.0 + jnp.tanh(0.7978845608028654 * (x + 0.044715 * x * x * x)))
 
 
-def kernel(tm, spaces, u_ref, f_ref, wd_ref, kt_ref, wp_ref, wu_ref, ends_ref,
-           wdb, wub, wcs, snd0, nrt0, sth0, snd, nrt, sth, send_sem, recv_sem):
+def kernel(tm, spaces, ens, u_hbm, f_hbm, wd_hbm, dk_hbm, wp_hbm, wu_hbm, out_ref, mean_ref,
+           u_in, f_in, wd_ref, dk_ref, wp_ref, wu_ref,
+           wdb, wub, wcs, snd0, nrt0, sth0, snd, nrt, sth,
+           ebuf, parts, mbuf, got, got_mean,
+           load_sem, send_sem, recv_sem, end_send, end_recv, part_send, part_recv, mean_send, mean_recv):
+    loads = []
+    for i, (src, dst) in enumerate([(u_hbm, u_in), (f_hbm, f_in), (wd_hbm, wd_ref), (dk_hbm, dk_ref),
+                                    (wp_hbm, wp_ref), (wu_hbm, wu_ref)]):
+        loads.append(pltpu.make_async_copy(src, dst, load_sem.at[i]))
+    for c in loads:
+        c.start()
+    u_ref, f_ref = u_in.at[0], f_in
+    e = lax.axis_index("ens")
     t = lax.axis_index("tm")
     s = lax.axis_index("space")
     fields, half, columns = u_ref.shape
@@ -115,6 +128,8 @@
             picked = jnp.where(pos == k, ref[:, k * block : (k + 1) * block, :], picked)
         return picked
 
+    loads[0].wait()
+    loads[1].wait()
     r_i, c_i = iota((columns, columns), 0), iota((columns, columns), 1)
     odd = jnp.where(c_i >= cols, 1, 0)
     to_parity = jnp.where(r_i == 2 * (c_i - odd * cols) + odd, 1.0, 0.0).astype(BF16)
@@ -126,6 +141,8 @@
             snd0[2 * f + b] = moved[f, :, b * cols : (b + 1) * cols]
     copies = exchange(0, snd0, nrt0, sth0)
 
+    for c in loads[2:]:
+        c.wait()
     rows_in = 3 * block // 2
     wide = groups * padded
     for r in range(rows_in):
@@ -143,9 +160,10 @@
         wub[:, r * ch : (r + 1) * ch] = jnp.dot(sel, wu_ref[...], preferred_element_type=F32).astype(BF16)
     for l in range(layers):
         w = wp_ref[l].astype(F32)
+        taps = dk_ref[l].T
         for a in range(3):
             for b in range(3):
-                tap = kt_ref[l, 3 * a + b : 3 * a + b + 1, :]
+                tap = taps[3 * a + b : 3 * a + b + 1, :]
                 wcs[l, b * ch : (b + 1) * ch, a * ch : (a + 1) * ch] = (w * tap).astype(BF16)
 
     def coarse(own, state):
@@ -173,10 +191,76 @@
     odd_j = jnp.where(r_j >= cols, 1, 0)
     from_parity = jnp.where(c_j == 2 * (r_j - odd_j * cols) + odd_j, 1.0, 0.0).astype(BF16)
 
+    chunk = fields // ens
+
     def finish(n, end):
         pieces = [jnp.concatenate([end[2 * f], end[2 * f + 1]], axis=1) for f in range(fields)]
         flat = jnp.concatenate(pieces, axis=0)
-        ends_ref[n] = exact_move(flat, from_parity).reshape(fields, block, columns)
+        ebuf[n] = exact_move(flat, from_parity).reshape(fields, block, columns)
+        for d in range(1, ens):
+            part_copy(n, d).start()
+
+        @pl.when(t != n)
+        def _():
+            end_copy(n).start()
+
+    def part_copy(n, d):
+        other = lax.rem(e + d, ens)
+        return pltpu.make_async_remote_copy(
+            ebuf.at[n, pl.ds(other * chunk, chunk)], parts.at[n, d - 1], part_send.at[n, d - 1], part_recv.at[n, d - 1],
+            device_id={"ens": other}, device_id_type=MESH)
+
+    def end_copy(n):
+        return pltpu.make_async_remote_copy(
+            ebuf.at[n], got.at[pos], end_send.at[n], end_recv.at[t],
+            device_id={"tm": n}, device_id_type=MESH)
+
+    def mean_copy(n, d):
+        return pltpu.make_async_remote_copy(
+            mbuf.at[n], got_mean.at[pos, d], mean_send.at[n, d], mean_recv.at[t, d],
+            device_id={"tm": n, "ens": lax.rem(e + d, ens)}, device_id_type=MESH)
+
+    def reduce(n):
+        acc = ebuf[n, pl.ds(e * chunk, chunk)]
+        for d in range(1, ens):
+            part_copy(n, d).wait()
+            acc = acc + parts[n, d - 1]
+        mbuf[n] = acc * (1.0 / ens)
+        for d in range(1, ens):
+            mean_copy(n, d).start()
+
+        @pl.when(t != n)
+        def _():
+            mean_copy(n, 0).start()
+
+    def collect():
+        for n in range(tm):
+            @pl.when(t != n)
+            def _():
+                end_copy(n).wait_send()
+                mean_copy(n, 0).wait_send()
+                pltpu.make_async_remote_copy(
+                    ebuf.at[n], got.at[swap_order(n)], end_send.at[n], end_recv.at[n],
+                    device_id={"tm": n}, device_id_type=MESH).wait_recv()
+                pltpu.make_async_remote_copy(
+                    mbuf.at[n], got_mean.at[swap_order(n), 0], mean_send.at[n, 0], mean_recv.at[n, 0],
+                    device_id={"tm": n}, device_id_type=MESH).wait_recv()
+
+            @pl.when(t == n)
+            def _():
+                got[swap_order(n)] = ebuf[n]
+                got_mean[swap_order(n), 0] = mbuf[n]
+
+            for d in range(1, ens):
+                mean_copy(n, d).wait_send()
+                pltpu.make_async_remote_copy(
+                    mbuf.at[n], got_mean.at[swap_order(n), d], mean_send.at[n, d], mean_recv.at[n, d],
+                    device_id={"ens": lax.rem(e + d, ens)}, device_id_type=MESH).wait_recv()
+        for p in range(tm):
+            out_ref[:, p * block : (p + 1) * block, :] = got[p]
+            for d in range(ens):
+                first = lax.rem(e + ens - d, ens) * chunk
+                mean_ref[pl.ds(first, chunk), p * block : (p + 1) * block, :] = got_mean[p, d]
 
     def next_stage(stage, starts):
         for i, start in enumerate(starts):
@@ -209,6 +293,7 @@
     w2 = gv1 + (fine(v1p) - gv1)
     moving = next_stage(2, [u2, v2, w2])
     finish(1, w2)
+    reduce(0)
     u2p, v2p, w2p = arrived(2, moving, [u2, v2, w2])
 
     gu2 = coarse(u2, u2p)
@@ -218,30 +303,37 @@
     w3 = gw2 + (fine(v2p) - gv2)
     moving = next_stage(3, [v3, w3])
     finish(2, w3)
+    reduce(1)
     v3p, w3p = arrived(3, moving, [v3, w3])
 
     gv3 = coarse(v3, v3p)
     gw3 = coarse(w3, w3p)
     finish(3, gw3 + (fine(v3p) - gv3))
+    reduce(2)
+    reduce(3)
+    collect()
 
 
 def local(initial_state, forcing, w_down, depth_kernel, w_point, w_up):
-    tm, spaces = lax.axis_size("tm"), lax.axis_size("space")
+    tm, spaces, ens = lax.axis_size("tm"), lax.axis_size("space"), lax.axis_size("ens")
     _, fields, half, columns = initial_state.shape
     block = half // tm
     cols, groups = columns // 2, 2 * fields
     layers, ch, _ = depth_kernel.shape
     assert block == FINE == 2 * layers and tm == 4
-    taps = jnp.swapaxes(depth_kernel, 1, 2)
+    assert fields % ens == 0
     count = groups + 2 * forcing.shape[0]
+    chunk = fields // ens
     vmem = pl.BlockSpec(memory_space=pltpu.VMEM)
-    ends = pl.pallas_call(
-        lambda *refs: kernel(tm, spaces, *refs),
+    hbm = pl.BlockSpec(memory_space=pl.ANY)
+    args = (initial_state, forcing, w_down, depth_kernel, w_point, w_up)
+    ending, mean = pl.pallas_call(
+        lambda *refs: kernel(tm, spaces, ens, *refs),
         name="parareal",
-        out_shape=jax.ShapeDtypeStruct((tm, fields, block, columns), F32),
-        in_specs=[vmem] * 6,
-        out_specs=vmem,
-        scratch_shapes=[
+        out_shape=[jax.ShapeDtypeStruct((fields, half, columns), F32)] * 2,
+        in_specs=[hbm] * 6,
+        out_specs=[vmem] * 2,
+        scratch_shapes=[pltpu.VMEM(a.shape, a.dtype) for a in args] + [
             pltpu.VMEM((3 * block // 2 * ch, groups * 4 * block), BF16),
             pltpu.VMEM((groups * block, block // 2 * ch), BF16),
             pltpu.VMEM((layers, 3 * ch, 3 * ch), BF16),
@@ -251,15 +343,23 @@
             pltpu.VMEM((3, 3, groups, block, cols), F32),
             pltpu.VMEM((3, 3, groups, block, cols), F32),
             pltpu.VMEM((3, 3, groups, block, cols), F32),
+            pltpu.VMEM((tm, fields, block, columns), F32),
+            pltpu.VMEM((tm, max(ens - 1, 1), chunk, block, columns), F32),
+            pltpu.VMEM((tm, chunk, block, columns), F32),
+            pltpu.VMEM((tm, fields, block, columns), F32),
+            pltpu.VMEM((tm, ens, chunk, block, columns), F32),
+            pltpu.SemaphoreType.DMA((6,)),
             pltpu.SemaphoreType.DMA((4, 2)),
             pltpu.SemaphoreType.DMA((4, 2)),
+            pltpu.SemaphoreType.DMA((tm,)),
+            pltpu.SemaphoreType.DMA((tm,)),
+            pltpu.SemaphoreType.DMA((tm, max(ens - 1, 1))),
+            pltpu.SemaphoreType.DMA((tm, max(ens - 1, 1))),
+            pltpu.SemaphoreType.DMA((tm, ens)),
+            pltpu.SemaphoreType.DMA((tm, ens)),
         ],
         compiler_params=pltpu.CompilerParams(has_side_effects=True, vmem_limit_bytes=32 << 20),
-    )(initial_state[0], forcing, w_down, taps, w_point, w_up)
-    gathered = lax.all_to_all(ends, "tm", 0, 0)
-    order = jnp.stack([gathered[p] for p in (0, 1, 3, 2)], axis=1)
-    ending = order.reshape(fields, half, columns)
-    mean = lax.psum(ending, "ens") / lax.axis_size("ens")
+    )(*args)
     return ending[None, None], mean[None]
 
 

time: 101 us -> 48.9 us (0.48); the launches traced: 99.3 us -> 48.7 us
  waiting for transfers between devices: 39.3 us -> 0 us
  between operations: 14.1 us -> 0.67 us
  Pallas kernels: 32.8 us -> 43.5 us
  blocking collectives: 6.79 us -> 0 us
    psum x1 -> x0, waiting for transfers between devices: 38.6 us -> none  [local(): mean = lax.psum(ending, 'ens') / lax.axis_size('ens')]
    pallas_call x1, Pallas kernels: 32.8 us -> 43.5 us  [local(): pl.pallas_call(lambda *refs: kernel(tm, spaces, ens, *refs), name='parare...]
    all_to_all x1 -> x0, blocking collectives: 6.79 us -> none  [local(): gathered = lax.all_to_all(ends, 'tm', 0, 0)]
  transfers between devices with their start and end apart: 1 -> 0, of which waited for: 1 -> 0; matrix products, arithmetic and copies ran while one was open for 0% -> 0% of each run, Pallas kernels for 0% -> 0%
where the time goes in v1:
time: 48.9 us; the launch traced here: 48.7 us
  Pallas kernels  43.5 us (89%)
  local copies, waits for them, and re-layouts  4.53 us (9%)
  between operations  0.67 us (1%)
    pallas_call x1, Pallas kernels, local(): pl.pallas_call(lambda *refs: kernel(tm, spaces, ens, *refs), name='parare...  43.5 us
    unnamed x14, local copies, waits for them, and re-layouts  4.53 us

profile of v1, /device:TPU:6, one launch (start us, length us, event | category | flops | bytes accessed | tf_op | source)
XLA Modules:
  0.0 48.7 jit_solution(11605002302851751151)
XLA Ops:
  0.6 0.0 copy-start.4
  0.6 0.0 copy-start
  0.6 0.8 %copy.8.refs_2_ = bf16[128,16]{1,0:T(8,128)(2,1)S(1)} copy(bf16[128,16]{0,1:T(8,128)(2,1)} %param.8) | data formatting | bytes 8192 | tf_op args[2]
  1.5 0.0 copy-done.4
  1.5 0.0 copy-start.3
  1.5 0.1 copy.9.refs_3_
  1.6 0.0 copy-done
  1.6 0.6 %copy-done.3 = bf16[16,128]{1,0:T(8,128)(2,1)S(1)} copy-done((bf16[16,128]{1,0:T(8,128)(2,1)S(1)}, bf16[16,128]{1,0:T(8,128)(2,1)}, u32[]{:S(2)}) %copy-start.3) | copy-done | bytes 4120
  2.2 0.0 copy-start.1
  2.2 0.8 %copy-done.1 = f32[2,16,512]{2,1,0:T(8,128)S(1)} copy-done((f32[2,16,512]{2,1,0:T(8,128)S(1)}, f32[2,16,512]{2,1,0:T(8,128)}, u32[]{:S(2)}) %copy-start.1) | copy-done | bytes 65560
  3.0 0.0 copy-start.2
  3.0 0.8 %copy-done.2 = bf16[2,128,128]{2,1,0:T(8,128)(2,1)S(1)} copy-done((bf16[2,128,128]{2,1,0:T(8,128)(2,1)S(1)}, bf16[2,128,128]{2,1,0:T(8,128)(2,1)}, u32[]{:S(2)}) %copy-start.2) | copy-done | bytes 65560
  3.9 43.5 %parareal.1 = (f32[4,16,512]{2,1,0:T(8,128)S(1)}, f32[4,16,512]{2,1,0:T(8,128)S(1)}) custom-call(f32[1,4,16,512]{3,2,1,0:T(8,128)S(1)} %copy-done, f32[2,16,512]{2,1,0:T(8,128)S(1)} %copy-done.1, bf16[128,16]{1,0:T(8,128)(2,1)S(1)} %copy.8.refs_2_, f32[2,128,9]{2,1,0:T(8,128)S(1)} %copy.9.refs_3_, bf16[2,128,128]{2,1,0:T(8,128)(2,1)S(1)} %copy-done.2, ...), custom_call_target="tpu_custom_call" | custom-call | tf_op jit(solution)/shard_map/parareal/pallas_call | solution.py:330
  47.4 0.7 %copy.12 = f32[1,1,4,16,512]{4,3,2,1,0:T(8,128)} copy(f32[1,1,4,16,512]{4,3,2,1,0:T(8,128)S(1)} %bitcast.3) | data formatting | bytes 262144
  48.0 0.7 %copy.13 = f32[1,4,16,512]{3,2,1,0:T(8,128)} copy(f32[1,4,16,512]{3,2,1,0:T(8,128)S(1)} %bitcast.2) | data formatting | bytes 262144
Async XLA Ops:
  0.6 0.9 %copy-start.4 = (f32[2,128,9]{1,0,2:T(2,128)S(1)}, f32[2,128,9]{1,0,2:T(2,128)}, u32[]{:S(2)}) copy-start(f32[2,128,9]{1,0,2:T(2,128)} %param.9) | copy-start | bytes 27652
  0.6 1.0 %copy-start = (f32[1,4,16,512]{3,2,1,0:T(8,128)S(1)}, f32[1,4,16,512]{3,2,1,0:T(8,128)}, u32[]{:S(2)}) copy-start(f32[1,4,16,512]{3,2,1,0:T(8,128)} %refs_0_.1) | copy-start | bytes 393220
  1.5 0.7 %copy-start.3 = (bf16[16,128]{1,0:T(8,128)(2,1)S(1)}, bf16[16,128]{1,0:T(8,128)(2,1)}, u32[]{:S(2)}) copy-start(bf16[16,128]{1,0:T(8,128)(2,1)} %refs_5_.1) | copy-start | bytes 12292
  2.2 0.8 %copy-start.1 = (f32[2,16,512]{2,1,0:T(8,128)S(1)}, f32[2,16,512]{2,1,0:T(8,128)}, u32[]{:S(2)}) copy-start(f32[2,16,512]{2,1,0:T(8,128)} %refs_1_.1) | copy-start | bytes 196612
  3.0 0.8 %copy-start.2 = (bf16[2,128,128]{2,1,0:T(8,128)(2,1)S(1)}, bf16[2,128,128]{2,1,0:T(8,128)(2,1)}, u32[]{:S(2)}) copy-start(bf16[2,128,128]{2,1,0:T(8,128)(2,1)} %refs_4_.1) | copy-start | bytes 196612

commit v2 on v1

--- a/solution.py
+++ b/solution.py
@@ -128,6 +128,11 @@
             picked = jnp.where(pos == k, ref[:, k * block : (k + 1) * block, :], picked)
         return picked
 
+    barrier = pltpu.get_barrier_semaphore()
+    peers = neighbours + [{"tm": lax.rem(t + i, tm), "ens": lax.rem(e + j, ens)}
+                          for i in range(tm) for j in range(ens) if i + j > 0]
+    for peer in peers:
+        pl.semaphore_signal(barrier, inc=1, device_id=peer, device_id_type=MESH)
     loads[0].wait()
     loads[1].wait()
     r_i, c_i = iota((columns, columns), 0), iota((columns, columns), 1)
@@ -136,9 +141,13 @@
     both = jnp.concatenate([own_rows(u_ref), own_rows(f_ref)], axis=0)
     count = fields + f_ref.shape[0]
     moved = exact_move(both.reshape(count * block, columns), to_parity).reshape(count, block, columns)
+    first = []
     for f in range(count):
         for b in (0, 1):
-            snd0[2 * f + b] = moved[f, :, b * cols : (b + 1) * cols]
+            first.append(moved[f, :, b * cols : (b + 1) * cols])
+    first = jnp.stack(first)
+    snd0[...] = first.reshape(2 * count * block, cols).astype(snd0.dtype)
+    pl.semaphore_wait(barrier, len(peers))
     copies = exchange(0, snd0, nrt0, sth0)
 
     for c in loads[2:]:
@@ -184,6 +193,9 @@
     def fine(state):
         return fine_sweep(state, force)[:, block : 2 * block]
 
+    def unpack(x):
+        return x.astype(F32).reshape(-1, block, cols)
+
     def pad(north, own, south):
         return jnp.concatenate([north, own, south, jnp.zeros_like(own)], axis=1)
 
@@ -264,20 +276,20 @@
 
     def next_stage(stage, starts):
         for i, start in enumerate(starts):
-            snd[stage - 1, i] = start
+            snd[stage - 1, i] = start.reshape(groups * block, cols).astype(snd.dtype)
         k = len(starts)
         return exchange(stage, snd.at[stage - 1, 0:k], nrt.at[stage - 1, 0:k], sth.at[stage - 1, 0:k])
 
     def arrived(stage, moving, starts):
         for c in moving:
             c.wait()
-        return [pad(nrt[stage - 1, i], start, sth[stage - 1, i]) for i, start in enumerate(starts)]
+        return [pad(unpack(nrt[stage - 1, i]), start, unpack(sth[stage - 1, i])) for i, start in enumerate(starts)]
 
     for c in copies:
         c.wait()
-    everything = pad(nrt0[...], snd0[...], sth0[...])
+    everything = pad(unpack(nrt0[...]), first, unpack(sth0[...]))
     force = everything[groups:]
-    start0 = snd0[0:groups]
+    start0 = first[:groups]
     state0 = everything[:groups]
 
     g0 = coarse(start0, state0)
@@ -325,7 +337,7 @@
     count = groups + 2 * forcing.shape[0]
     chunk = fields // ens
     vmem = pl.BlockSpec(memory_space=pltpu.VMEM)
-    hbm = pl.BlockSpec(memory_space=pl.ANY)
+    hbm = pl.BlockSpec(memory_space=pltpu.HBM)
     args = (initial_state, forcing, w_down, depth_kernel, w_point, w_up)
     ending, mean = pl.pallas_call(
         lambda *refs: kernel(tm, spaces, ens, *refs),
@@ -337,12 +349,12 @@
             pltpu.VMEM((3 * block // 2 * ch, groups * 4 * block), BF16),
             pltpu.VMEM((groups * block, block // 2 * ch), BF16),
             pltpu.VMEM((layers, 3 * ch, 3 * ch), BF16),
-            pltpu.VMEM((count, block, cols), F32),
-            pltpu.VMEM((count, block, cols), F32),
-            pltpu.VMEM((count, block, cols), F32),
-            pltpu.VMEM((3, 3, groups, block, cols), F32),
-            pltpu.VMEM((3, 3, groups, block, cols), F32),
-            pltpu.VMEM((3, 3, groups, block, cols), F32),
+            pltpu.VMEM((count * block, cols), BF16),
+            pltpu.VMEM((count * block, cols), BF16),
+            pltpu.VMEM((count * block, cols), BF16),
+            pltpu.VMEM((3, 3, groups * block, cols), BF16),
+            pltpu.VMEM((3, 3, groups * block, cols), BF16),
+            pltpu.VMEM((3, 3, groups * block, cols), BF16),
             pltpu.VMEM((tm, fields, block, columns), F32),
             pltpu.VMEM((tm, max(ens - 1, 1), chunk, block, columns), F32),
             pltpu.VMEM((tm, chunk, block, columns), F32),
@@ -358,7 +370,7 @@
             pltpu.SemaphoreType.DMA((tm, ens)),
             pltpu.SemaphoreType.DMA((tm, ens)),
         ],
-        compiler_params=pltpu.CompilerParams(has_side_effects=True, vmem_limit_bytes=32 << 20),
+        compiler_params=pltpu.CompilerParams(has_side_effects=True, collective_id=0, vmem_limit_bytes=32 << 20),
     )(*args)
     return ending[None, None], mean[None]
 

time: 48.9 us -> 44.4 us (0.908)
  Pallas kernels: 43.5 us -> 38.9 us
    pallas_call x1, Pallas kernels: 43.5 us -> 38.9 us  [local(): pl.pallas_call(lambda *refs: kernel(tm, spaces, ens, *refs), name='parare...]
where the time goes in v2:
time: 44.4 us; the launch traced here: 44.1 us
  Pallas kernels  38.9 us (88%)
  local copies, waits for them, and re-layouts  4.53 us (10%)
  between operations  0.67 us (2%)
    pallas_call x1, Pallas kernels, local(): pl.pallas_call(lambda *refs: kernel(tm, spaces, ens, *refs), name='parare...  38.9 us
    unnamed x14, local copies, waits for them, and re-layouts  4.53 us

profile of v2, /device:TPU:6, one launch (start us, length us, event | category | flops | bytes accessed | tf_op | source)
XLA Modules:
  0.0 44.1 jit_solution(16389047633646256634)
XLA Ops:
  0.6 0.0 copy-start.4
  0.6 0.0 copy-start
  0.6 0.8 %copy.8.refs_2_ = bf16[128,16]{1,0:T(8,128)(2,1)S(1)} copy(bf16[128,16]{0,1:T(8,128)(2,1)} %param.8) | data formatting | bytes 8192 | tf_op args[2]
  1.5 0.0 copy-done.4
  1.5 0.0 copy-start.3
  1.5 0.1 copy.9.refs_3_
  1.6 0.0 copy-done
  1.6 0.6 %copy-done.3 = bf16[16,128]{1,0:T(8,128)(2,1)S(1)} copy-done((bf16[16,128]{1,0:T(8,128)(2,1)S(1)}, bf16[16,128]{1,0:T(8,128)(2,1)}, u32[]{:S(2)}) %copy-start.3) | copy-done | bytes 4120
  2.2 0.0 copy-start.1
  2.2 0.8 %copy-done.1 = f32[2,16,512]{2,1,0:T(8,128)S(1)} copy-done((f32[2,16,512]{2,1,0:T(8,128)S(1)}, f32[2,16,512]{2,1,0:T(8,128)}, u32[]{:S(2)}) %copy-start.1) | copy-done | bytes 65560
  3.0 0.0 copy-start.2
  3.0 0.8 %copy-done.2 = bf16[2,128,128]{2,1,0:T(8,128)(2,1)S(1)} copy-done((bf16[2,128,128]{2,1,0:T(8,128)(2,1)S(1)}, bf16[2,128,128]{2,1,0:T(8,128)(2,1)}, u32[]{:S(2)}) %copy-start.2) | copy-done | bytes 65560
  3.9 38.9 %parareal.1 = (f32[4,16,512]{2,1,0:T(8,128)S(1)}, f32[4,16,512]{2,1,0:T(8,128)S(1)}) custom-call(f32[1,4,16,512]{3,2,1,0:T(8,128)S(1)} %copy-done, f32[2,16,512]{2,1,0:T(8,128)S(1)} %copy-done.1, bf16[128,16]{1,0:T(8,128)(2,1)S(1)} %copy.8.refs_2_, f32[2,128,9]{2,1,0:T(8,128)S(1)} %copy.9.refs_3_, bf16[2,128,128]{2,1,0:T(8,128)(2,1)S(1)} %copy-done.2, ...), custom_call_target="tpu_custom_call" | custom-call | tf_op jit(solution)/shard_map/parareal/pallas_call | solution.py:342
  42.8 0.7 %copy.12 = f32[1,1,4,16,512]{4,3,2,1,0:T(8,128)} copy(f32[1,1,4,16,512]{4,3,2,1,0:T(8,128)S(1)} %bitcast.3) | data formatting | bytes 262144
  43.4 0.7 %copy.13 = f32[1,4,16,512]{3,2,1,0:T(8,128)} copy(f32[1,4,16,512]{3,2,1,0:T(8,128)S(1)} %bitcast.2) | data formatting | bytes 262144
Async XLA Ops:
  0.6 0.9 %copy-start.4 = (f32[2,128,9]{1,0,2:T(2,128)S(1)}, f32[2,128,9]{1,0,2:T(2,128)}, u32[]{:S(2)}) copy-start(f32[2,128,9]{1,0,2:T(2,128)} %param.9) | copy-start | bytes 27652
  0.6 1.0 %copy-start = (f32[1,4,16,512]{3,2,1,0:T(8,128)S(1)}, f32[1,4,16,512]{3,2,1,0:T(8,128)}, u32[]{:S(2)}) copy-start(f32[1,4,16,512]{3,2,1,0:T(8,128)} %refs_0_.1) | copy-start | bytes 393220
  1.5 0.7 %copy-start.3 = (bf16[16,128]{1,0:T(8,128)(2,1)S(1)}, bf16[16,128]{1,0:T(8,128)(2,1)}, u32[]{:S(2)}) copy-start(bf16[16,128]{1,0:T(8,128)(2,1)} %refs_5_.1) | copy-start | bytes 12292
  2.2 0.8 %copy-start.1 = (f32[2,16,512]{2,1,0:T(8,128)S(1)}, f32[2,16,512]{2,1,0:T(8,128)}, u32[]{:S(2)}) copy-start(f32[2,16,512]{2,1,0:T(8,128)} %refs_1_.1) | copy-start | bytes 196612
  3.0 0.8 %copy-start.2 = (bf16[2,128,128]{2,1,0:T(8,128)(2,1)S(1)}, bf16[2,128,128]{2,1,0:T(8,128)(2,1)}, u32[]{:S(2)}) copy-start(bf16[2,128,128]{2,1,0:T(8,128)(2,1)} %refs_4_.1) | copy-start | bytes 196612

commit v3 on v2

--- a/solution.py
+++ b/solution.py
@@ -84,7 +84,7 @@
            u_in, f_in, wd_ref, dk_ref, wp_ref, wu_ref,
            wdb, wub, wcs, snd0, nrt0, sth0, snd, nrt, sth,
            ebuf, parts, mbuf, got, got_mean,
-           load_sem, send_sem, recv_sem, end_send, end_recv, part_send, part_recv, mean_send, mean_recv):
+           load_sem, send_sem, recv_sem, end_send, end_recv, part_send, part_recv, mean_send, mean_recv, reach):
     loads = []
     for i, (src, dst) in enumerate([(u_hbm, u_in), (f_hbm, f_in), (wd_hbm, wd_ref), (dk_hbm, dk_ref),
                                     (wp_hbm, wp_ref), (wu_hbm, wu_ref)]):
@@ -129,8 +129,8 @@
         return picked
 
     barrier = pltpu.get_barrier_semaphore()
-    peers = neighbours + [{"tm": lax.rem(t + i, tm), "ens": lax.rem(e + j, ens)}
-                          for i in range(tm) for j in range(ens) if i + j > 0]
+    same_rows = [{"tm": lax.rem(t + i, tm)} for i in range(1, tm)]
+    peers = neighbours + same_rows + [{"ens": lax.rem(e + i, ens)} for i in range(1, ens)]
     for peer in peers:
         pl.semaphore_signal(barrier, inc=1, device_id=peer, device_id_type=MESH)
     loads[0].wait()
@@ -148,6 +148,8 @@
     first = jnp.stack(first)
     snd0[...] = first.reshape(2 * count * block, cols).astype(snd0.dtype)
     pl.semaphore_wait(barrier, len(peers))
+    for peer in same_rows:
+        pl.semaphore_signal(reach, inc=1, device_id=peer, device_id_type=MESH)
     copies = exchange(0, snd0, nrt0, sth0)
 
     for c in loads[2:]:
@@ -305,6 +307,7 @@
     w2 = gv1 + (fine(v1p) - gv1)
     moving = next_stage(2, [u2, v2, w2])
     finish(1, w2)
+    pl.semaphore_wait(reach, len(same_rows))
     reduce(0)
     u2p, v2p, w2p = arrived(2, moving, [u2, v2, w2])
 
@@ -369,6 +372,7 @@
             pltpu.SemaphoreType.DMA((tm, max(ens - 1, 1))),
             pltpu.SemaphoreType.DMA((tm, ens)),
             pltpu.SemaphoreType.DMA((tm, ens)),
+            pltpu.SemaphoreType.REGULAR,
         ],
         compiler_params=pltpu.CompilerParams(has_side_effects=True, collective_id=0, vmem_limit_bytes=32 << 20),
     )(*args)

time: 44.4 us -> 43.4 us (0.977)
  Pallas kernels: 38.9 us -> 38 us
    pallas_call x1, Pallas kernels: 38.9 us -> 38 us  [local(): pl.pallas_call(lambda *refs: kernel(tm, spaces, ens, *refs), name='parare...]
where the time goes in v3:
time: 43.4 us; the launch traced here: 43.2 us
  Pallas kernels  38 us (88%)
  local copies, waits for them, and re-layouts  4.53 us (10%)
  between operations  0.67 us (2%)
    pallas_call x1, Pallas kernels, local(): pl.pallas_call(lambda *refs: kernel(tm, spaces, ens, *refs), name='parare...  38 us
    unnamed x14, local copies, waits for them, and re-layouts  4.53 us

profile of v3, /device:TPU:6, one launch (start us, length us, event | category | flops | bytes accessed | tf_op | source)
XLA Modules:
  0.0 43.2 jit_solution(15061406828491434249)
XLA Ops:
  0.6 0.0 copy-start.4
  0.6 0.0 copy-start
  0.6 0.8 %copy.8.refs_2_ = bf16[128,16]{1,0:T(8,128)(2,1)S(1)} copy(bf16[128,16]{0,1:T(8,128)(2,1)} %param.8) | data formatting | bytes 8192 | tf_op args[2]
  1.5 0.0 copy-done.4
  1.5 0.0 copy-start.3
  1.5 0.1 copy.9.refs_3_
  1.6 0.0 copy-done
  1.6 0.6 %copy-done.3 = bf16[16,128]{1,0:T(8,128)(2,1)S(1)} copy-done((bf16[16,128]{1,0:T(8,128)(2,1)S(1)}, bf16[16,128]{1,0:T(8,128)(2,1)}, u32[]{:S(2)}) %copy-start.3) | copy-done | bytes 4120
  2.2 0.0 copy-start.1
  2.2 0.8 %copy-done.1 = f32[2,16,512]{2,1,0:T(8,128)S(1)} copy-done((f32[2,16,512]{2,1,0:T(8,128)S(1)}, f32[2,16,512]{2,1,0:T(8,128)}, u32[]{:S(2)}) %copy-start.1) | copy-done | bytes 65560
  3.0 0.0 copy-start.2
  3.0 0.8 %copy-done.2 = bf16[2,128,128]{2,1,0:T(8,128)(2,1)S(1)} copy-done((bf16[2,128,128]{2,1,0:T(8,128)(2,1)S(1)}, bf16[2,128,128]{2,1,0:T(8,128)(2,1)}, u32[]{:S(2)}) %copy-start.2) | copy-done | bytes 65560
  3.9 38.0 %parareal.1 = (f32[4,16,512]{2,1,0:T(8,128)S(1)}, f32[4,16,512]{2,1,0:T(8,128)S(1)}) custom-call(f32[1,4,16,512]{3,2,1,0:T(8,128)S(1)} %copy-done, f32[2,16,512]{2,1,0:T(8,128)S(1)} %copy-done.1, bf16[128,16]{1,0:T(8,128)(2,1)S(1)} %copy.8.refs_2_, f32[2,128,9]{2,1,0:T(8,128)S(1)} %copy.9.refs_3_, bf16[2,128,128]{2,1,0:T(8,128)(2,1)S(1)} %copy-done.2, ...), custom_call_target="tpu_custom_call" | custom-call | tf_op jit(solution)/shard_map/parareal/pallas_call | solution.py:345
  41.8 0.7 %copy.12 = f32[1,1,4,16,512]{4,3,2,1,0:T(8,128)} copy(f32[1,1,4,16,512]{4,3,2,1,0:T(8,128)S(1)} %bitcast.3) | data formatting | bytes 262144
  42.5 0.7 %copy.13 = f32[1,4,16,512]{3,2,1,0:T(8,128)} copy(f32[1,4,16,512]{3,2,1,0:T(8,128)S(1)} %bitcast.2) | data formatting | bytes 262144
Async XLA Ops:
  0.6 0.9 %copy-start.4 = (f32[2,128,9]{1,0,2:T(2,128)S(1)}, f32[2,128,9]{1,0,2:T(2,128)}, u32[]{:S(2)}) copy-start(f32[2,128,9]{1,0,2:T(2,128)} %param.9) | copy-start | bytes 27652
  0.6 1.0 %copy-start = (f32[1,4,16,512]{3,2,1,0:T(8,128)S(1)}, f32[1,4,16,512]{3,2,1,0:T(8,128)}, u32[]{:S(2)}) copy-start(f32[1,4,16,512]{3,2,1,0:T(8,128)} %refs_0_.1) | copy-start | bytes 393220
  1.5 0.7 %copy-start.3 = (bf16[16,128]{1,0:T(8,128)(2,1)S(1)}, bf16[16,128]{1,0:T(8,128)(2,1)}, u32[]{:S(2)}) copy-start(bf16[16,128]{1,0:T(8,128)(2,1)} %refs_5_.1) | copy-start | bytes 12292
  2.2 0.8 %copy-start.1 = (f32[2,16,512]{2,1,0:T(8,128)S(1)}, f32[2,16,512]{2,1,0:T(8,128)}, u32[]{:S(2)}) copy-start(f32[2,16,512]{2,1,0:T(8,128)} %refs_1_.1) | copy-start | bytes 196612
  3.0 0.8 %copy-start.2 = (bf16[2,128,128]{2,1,0:T(8,128)(2,1)S(1)}, bf16[2,128,128]{2,1,0:T(8,128)(2,1)}, u32[]{:S(2)}) copy-start(bf16[2,128,128]{2,1,0:T(8,128)(2,1)} %refs_4_.1) | copy-start | bytes 196612

commit v4 on v3

--- a/solution.py
+++ b/solution.py
@@ -130,9 +130,13 @@
 
     barrier = pltpu.get_barrier_semaphore()
     same_rows = [{"tm": lax.rem(t + i, tm)} for i in range(1, tm)]
-    peers = neighbours + same_rows + [{"ens": lax.rem(e + i, ens)} for i in range(1, ens)]
+    peers = same_rows + [{"ens": lax.rem(e + i, ens)} for i in range(1, ens)]
     for peer in peers:
         pl.semaphore_signal(barrier, inc=1, device_id=peer, device_id_type=MESH)
+    for edge, across in ((0, to_north), (tm - 1, to_south)):
+        @pl.when(pos == edge)
+        def _():
+            pl.semaphore_signal(barrier, inc=1, device_id=across, device_id_type=MESH)
     loads[0].wait()
     loads[1].wait()
     r_i, c_i = iota((columns, columns), 0), iota((columns, columns), 1)
@@ -147,7 +151,7 @@
             first.append(moved[f, :, b * cols : (b + 1) * cols])
     first = jnp.stack(first)
     snd0[...] = first.reshape(2 * count * block, cols).astype(snd0.dtype)
-    pl.semaphore_wait(barrier, len(peers))
+    pl.semaphore_wait(barrier, len(peers) + jnp.where((pos == 0) | (pos == tm - 1), 1, 0))
     for peer in same_rows:
         pl.semaphore_signal(reach, inc=1, device_id=peer, device_id_type=MESH)
     copies = exchange(0, snd0, nrt0, sth0)

time: 43.4 us -> 43.4 us (level)
  no operation moved by 1% of the time
where the time goes in v4:
time: 43.4 us; the launch traced here: 43.1 us
  Pallas kernels  37.9 us (87%)
  local copies, waits for them, and re-layouts  4.53 us (10%)
  between operations  0.67 us (2%)
    pallas_call x1, Pallas kernels, local(): pl.pallas_call(lambda *refs: kernel(tm, spaces, ens, *refs), name='parare...  37.9 us
    unnamed x14, local copies, waits for them, and re-layouts  4.53 us

profile of v4, /device:TPU:6, one launch (start us, length us, event | category | flops | bytes accessed | tf_op | source)
XLA Modules:
  0.0 43.1 jit_solution(14502024391809527008)
XLA Ops:
  0.6 0.0 copy-start.4
  0.6 0.0 copy-start
  0.6 0.8 %copy.8.refs_2_ = bf16[128,16]{1,0:T(8,128)(2,1)S(1)} copy(bf16[128,16]{0,1:T(8,128)(2,1)} %param.8) | data formatting | bytes 8192 | tf_op args[2]
  1.5 0.0 copy-done.4
  1.5 0.0 copy-start.3
  1.5 0.1 copy.9.refs_3_
  1.6 0.0 copy-done
  1.6 0.6 %copy-done.3 = bf16[16,128]{1,0:T(8,128)(2,1)S(1)} copy-done((bf16[16,128]{1,0:T(8,128)(2,1)S(1)}, bf16[16,128]{1,0:T(8,128)(2,1)}, u32[]{:S(2)}) %copy-start.3) | copy-done | bytes 4120
  2.2 0.0 copy-start.1
  2.2 0.8 %copy-done.1 = f32[2,16,512]{2,1,0:T(8,128)S(1)} copy-done((f32[2,16,512]{2,1,0:T(8,128)S(1)}, f32[2,16,512]{2,1,0:T(8,128)}, u32[]{:S(2)}) %copy-start.1) | copy-done | bytes 65560
  3.0 0.0 copy-start.2
  3.0 0.8 %copy-done.2 = bf16[2,128,128]{2,1,0:T(8,128)(2,1)S(1)} copy-done((bf16[2,128,128]{2,1,0:T(8,128)(2,1)S(1)}, bf16[2,128,128]{2,1,0:T(8,128)(2,1)}, u32[]{:S(2)}) %copy-start.2) | copy-done | bytes 65560
  3.9 37.9 %parareal.1 = (f32[4,16,512]{2,1,0:T(8,128)S(1)}, f32[4,16,512]{2,1,0:T(8,128)S(1)}) custom-call(f32[1,4,16,512]{3,2,1,0:T(8,128)S(1)} %copy-done, f32[2,16,512]{2,1,0:T(8,128)S(1)} %copy-done.1, bf16[128,16]{1,0:T(8,128)(2,1)S(1)} %copy.8.refs_2_, f32[2,128,9]{2,1,0:T(8,128)S(1)} %copy.9.refs_3_, bf16[2,128,128]{2,1,0:T(8,128)(2,1)S(1)} %copy-done.2, ...), custom_call_target="tpu_custom_call" | custom-call | tf_op jit(solution)/shard_map/parareal/pallas_call | solution.py:349
  41.8 0.7 %copy.12 = f32[1,1,4,16,512]{4,3,2,1,0:T(8,128)} copy(f32[1,1,4,16,512]{4,3,2,1,0:T(8,128)S(1)} %bitcast.3) | data formatting | bytes 262144
  42.5 0.7 %copy.13 = f32[1,4,16,512]{3,2,1,0:T(8,128)} copy(f32[1,4,16,512]{3,2,1,0:T(8,128)S(1)} %bitcast.2) | data formatting | bytes 262144
Async XLA Ops:
  0.6 0.9 %copy-start.4 = (f32[2,128,9]{1,0,2:T(2,128)S(1)}, f32[2,128,9]{1,0,2:T(2,128)}, u32[]{:S(2)}) copy-start(f32[2,128,9]{1,0,2:T(2,128)} %param.9) | copy-start | bytes 27652
  0.6 1.0 %copy-start = (f32[1,4,16,512]{3,2,1,0:T(8,128)S(1)}, f32[1,4,16,512]{3,2,1,0:T(8,128)}, u32[]{:S(2)}) copy-start(f32[1,4,16,512]{3,2,1,0:T(8,128)} %refs_0_.1) | copy-start | bytes 393220
  1.5 0.7 %copy-start.3 = (bf16[16,128]{1,0:T(8,128)(2,1)S(1)}, bf16[16,128]{1,0:T(8,128)(2,1)}, u32[]{:S(2)}) copy-start(bf16[16,128]{1,0:T(8,128)(2,1)} %refs_5_.1) | copy-start | bytes 12292
  2.2 0.8 %copy-start.1 = (f32[2,16,512]{2,1,0:T(8,128)S(1)}, f32[2,16,512]{2,1,0:T(8,128)}, u32[]{:S(2)}) copy-start(f32[2,16,512]{2,1,0:T(8,128)} %refs_1_.1) | copy-start | bytes 196612
  3.0 0.8 %copy-start.2 = (bf16[2,128,128]{2,1,0:T(8,128)(2,1)S(1)}, bf16[2,128,128]{2,1,0:T(8,128)(2,1)}, u32[]{:S(2)}) copy-start(bf16[2,128,128]{2,1,0:T(8,128)(2,1)} %refs_4_.1) | copy-start | bytes 196612
